TPU v7x, 512 devices: a whole 4x8x8 slice. The times are simulated.
512 devices in a mesh: rows: 64 (over z, y), feat: 8 (over x, core).
Axes of the slice: x: 4, y: 8, z: 8, core: 2. Of those that a mesh axis runs over, the one named last changes fastest.
Arguments:
- bin_ids: int32 [512, 131072], P('feat', 'rows'), may hold values from 0 to 255
- leaf_ids: int32 [131072], P('rows'), may hold values from 0 to 63
- gradient: float32 [131072], P('rows'), may hold values from -6 to 6
- hessian: float32 [131072], P('rows'), may hold values from 0.01 to 0.25
- raw_feats: bfloat16 [131072, 64], P(('rows', 'feat')), may hold values from -6 to 6
- prior_score: float32 [131072], P(('rows', 'feat')), may hold values from -6 to 6
- elected: int32 [64, 64], P(None, 'feat'), may hold values from 0 to 63, as said below
Outputs:
- relative_gain: float32 [64, 64, 256], P('rows', 'feat')
- coefficients: float32 [64, 65], P('rows')
- new_score: float32 [131072], P(('rows', 'feat'))
Inputs may be any that keep to these rules, and one draw needn't show every extreme that they name: `elected`: within each row, each group's 8 entries are distinct feature numbers of that group.
All inputs are finite; a program needn't handle non-finite values.
Results may differ from a plain program's by a relative error of at most 0.0029.
Values sent between devices are 32-bit elements; how exact they have to be, the bound alone decides.
A program may use at most 64 MiB of HBM per device.

v0:
```python
import jax
import jax.numpy as jnp
from jax import lax
from jax.sharding import PartitionSpec as P

BINS = 256


SPLIT_REG = 1.0
RIDGE_REG = 1.0
SHRINKAGE = 0.3


def split_gains(hist_grad, hist_hess):
    left_grad = jnp.cumsum(hist_grad, axis=-1)
    left_hess = jnp.cumsum(hist_hess, axis=-1)
    total_grad = left_grad[..., -1:]
    total_hess = left_hess[..., -1:]
    right_grad = total_grad - left_grad
    first = left_grad * left_grad / (left_hess + SPLIT_REG)
    second = right_grad * right_grad / (total_hess - left_hess + SPLIT_REG)
    whole = total_grad * total_grad / (total_hess + SPLIT_REG)
    return first + second - whole


def solve_leaves(blocks):
    width = blocks.shape[2]
    system = blocks[:, :width, :] + RIDGE_REG * jnp.eye(width, dtype=blocks.dtype)
    target = blocks[:, width:, :]
    factor = jnp.linalg.cholesky(system)
    middle = lax.linalg.triangular_solve(
        factor, target, left_side=False, lower=True, transpose_a=True
    )
    answer = lax.linalg.triangular_solve(
        factor, middle, left_side=False, lower=True, transpose_a=False
    )
    return -answer[:, 0, :]


def body(bin_ids, leaf_ids, gradient, hessian, raw_feats, prior_score, elected):
    row_total = bin_ids.shape[1]
    leaf_total = elected.shape[0]
    slot_count = elected.shape[1]
    owned = leaf_total // lax.axis_size("rows")
    group_rows = row_total // lax.axis_size("feat")
    grad_round = gradient.astype(jnp.bfloat16)
    hess_round = hessian.astype(jnp.bfloat16)
    zero_value = jnp.zeros((), jnp.bfloat16)
    leaf_table = jnp.arange(leaf_total, dtype=jnp.int32)
    leaf_onehot = (leaf_ids[:, None] == leaf_table[None, :]).astype(jnp.float32)
    elected_cols = jnp.transpose(elected).astype(jnp.float32)
    picked = lax.dot_general(
        elected_cols, leaf_onehot, (((1,), (1,)), ((), ())), precision=lax.Precision.HIGHEST
    ).astype(jnp.int32)
    chosen = jnp.take_along_axis(bin_ids, picked, axis=0)
    bin_table = jnp.arange(BINS, dtype=jnp.int32)
    bin_onehot = (chosen[:, :, None] == bin_table[None, None, :]).astype(jnp.bfloat16)
    wanted = lax.broadcasted_iota(jnp.int32, (1, owned * lax.axis_size("rows")), 1)
    member = leaf_ids[:, None] == wanted
    grad_part = jnp.where(member, grad_round[:, None], zero_value)
    hess_part = jnp.where(member, hess_round[:, None], zero_value)
    weights = jnp.stack([grad_part, hess_part], axis=2).reshape(
        row_total, 2 * (owned * lax.axis_size("rows"))
    )
    product = lax.dot_general(
        weights, bin_onehot, (((0,), (1,)), ((), ())), preferred_element_type=jnp.float32
    )
    histogram = lax.psum_scatter(
        product.reshape(owned * lax.axis_size("rows"), 2, slot_count * BINS),
        "rows",
        scatter_dimension=0,
        tiled=True,
    )
    shaped = histogram.reshape(owned, 2, slot_count, BINS)
    gains = split_gains(shaped[:, 0], shaped[:, 1])
    local_best = jnp.max(gains, axis=(1, 2))
    best = lax.pmax(local_best, "feat")
    relative_gain = gains - best[:, None, None]
    group_start = lax.axis_index("feat") * group_rows
    leaf_sub = lax.dynamic_slice_in_dim(leaf_ids, group_start, group_rows)
    grad_sub = lax.dynamic_slice_in_dim(grad_round, group_start, group_rows)
    hess_sub = lax.dynamic_slice_in_dim(hessian, group_start, group_rows)
    unit_column = jnp.ones((group_rows, 1), jnp.bfloat16)
    augmented = jnp.concatenate([raw_feats, unit_column], axis=1)
    weighted = (hess_sub[:, None] * augmented.astype(jnp.float32)).astype(jnp.bfloat16)
    extended = jnp.concatenate([weighted, grad_sub[:, None]], axis=1)
    ext_width = extended.shape[1]
    wanted = lax.broadcasted_iota(jnp.int32, (1, owned * lax.axis_size("rows")), 1)
    member = leaf_sub[:, None] == wanted
    spread = jnp.where(member[:, :, None], extended[:, None, :], zero_value).reshape(
        group_rows, owned * lax.axis_size("rows") * ext_width
    )
    product = lax.dot_general(
        spread, augmented, (((0,), (0,)), ((), ())), preferred_element_type=jnp.float32
    )
    partial_blocks = lax.psum_scatter(
        product.reshape(owned * lax.axis_size("rows"), ext_width, ext_width - 1),
        "rows",
        scatter_dimension=0,
        tiled=True,
    )
    local_blocks = lax.psum(partial_blocks, "feat")
    coefficients = solve_leaves(local_blocks)
    all_coefs = lax.all_gather(coefficients, "rows", axis=0, tiled=True)
    sub_onehot = (leaf_sub[:, None] == leaf_table[None, :]).astype(jnp.float32)
    row_coefs = jnp.dot(sub_onehot, all_coefs, precision=lax.Precision.HIGHEST)
    new_score = prior_score + SHRINKAGE * jnp.sum(augmented.astype(jnp.float32) * row_coefs, axis=1)
    return (relative_gain, coefficients, new_score)


def solution(mesh):
    in_specs = (
        P("feat", "rows"),
        P("rows"),
        P("rows"),
        P("rows"),
        P(("rows", "feat"), None),
        P(("rows", "feat")),
        P(None, "feat"),
    )
    out_specs = (P("rows", "feat", None), P("rows", None), P(("rows", "feat")))
    return jax.shard_map(body, mesh=mesh, in_specs=in_specs, out_specs=out_specs, check_vma=False)
```

profile of v0, /device:TPU:6, one launch (start us, length us, event | category | flops | bytes accessed | tf_op | source)
XLA Modules:
  0.0 885.2 jit_solution(8825843172253596968)
XLA Ops:
  7.2 0.7 convert_element_type.36
  8.0 0.7 convert_element_type.37
  8.7 1.6 compare_select_fusion.2
  10.4 130.6 %gather_fusion = s32[16384]{0:T(1024)S(1)} fusion(s32[64,2048]{1,0:T(8,128)S(1)} %copy-done, s32[16384]{0:T(1024)S(1)} %bitcast.78), kind=kCustom, calls=%fused_computation | custom fusion | bytes 262144 | tf_op jit(solution)/shard_map/jit(take_along_axis)/gather | solution.py:55
  141.0 0.8 compare_select_fusion.1
  141.8 1.2 pad_maximum_fusion
  143.2 0.3 dot_general.21
  143.6 2.2 iota_compare_fusion
  145.8 3.0 fusion.3
  148.8 1.8 copy.14
  150.7 0.8 dynamic_slice.10
  151.8 2.1 select_n.54
  153.9 2.6 dot_general.25
  156.6 2.2 fusion.12
  158.8 0.6 fusion.18
  160.0 156.6 %all-reduce.6.cloned.1.call-done = f32[64,2,2048]{2,1,0:T(2,128)} async-done(((f32[64,2,2048]{2,1,0:T(2,128)}), f32[64,2,2048]{2,1,0:T(2,128)}) %all-reduce.6.cloned.1.call-update) | async-done | bytes 1048592
  316.6 1.4 constant_dynamic-slice_fusion
  318.0 0.6 reduce-window.16
  318.7 0.6 reduce-window.14
  319.8 0.7 fusion.17
  320.5 10.6 %pmax.7 = f32[]{:T(128)} all-reduce(f32[]{:T(128)} %get-tuple-element.6), channel_id=1, replica_groups=mesh['rows'=64,'feat'=8] {'feat'}, use_global_device_ids=true, to_apply=%region_6.7 | all-reduce | flops 1 | bytes 8 | tf_op jit(solution)/shard_map/pmax | solution.py:77
  331.1 1.2 broadcast_subtract_fusion
  332.4 233.7 %reduce-scatter.4.cloned.1.call-done = f32[1,66,65]{2,1,0:T(8,128)} async-done(((f32[64,66,65]{2,1,0:T(8,128)}), f32[1,66,65]{2,1,0:T(8,128)}) %reduce-scatter.4.cloned.1.call-update) | async-done | bytes 17176
  566.1 21.7 %psum.7 = f32[1,66,65]{2,1,0:T(8,128)S(1)} all-reduce(f32[1,66,65]{2,1,0:T(8,128)} %reduce-scatter.4.cloned.1.call-done), channel_id=1, replica_groups=mesh['rows'=64,'feat'=8] {'feat'}, use_global_device_ids=true, to_apply=%region_8.9 | all-reduce | flops 4290 | bytes 34320 | tf_op jit(solution)/shard_map/psum | solution.py:102
  587.9 5.9 custom-call.9
  593.9 0.6 compare_reduce_fusion
  594.5 0.7 fusion.8
  595.2 5.0 custom-call.10
  600.5 0.3 dynamic-update-slice.3
  600.8 276.6 %all-reduce.1 = f32[4160]{0:T(1024)S(1)} all-reduce(f32[4160]{0:T(1024)S(1)} %dynamic-update-slice.3), channel_id=2, replica_groups=mesh['rows'=64,'feat'=8] {'rows'}, use_global_device_ids=true, to_apply=%add.1 | all-reduce | flops 4160 | bytes 33280
  877.6 0.2 fusion.1
  877.8 0.6 multiply_add_fusion
  (46 shorter events, 2.1 us)
Async XLA Ops:
  7.2 3.2 copy-start
  7.2 309.4 %all-reduce.6.cloned.1.call-start = ((), (), s32[]{:S(2)}) async-start(), calls=%async_computation.1 | async-start | bytes 2097152
  10.4 130.6 %copy-start.2 = (s32[2048]{0:T(1024)S(1)}, s32[2048]{0:T(1024)}, u32[]{:S(2)}) copy-start(s32[2048]{0:T(1024)} %param.8) | copy-start | bytes 24580
  145.8 5.7 copy-start.1
  150.6 415.5 %reduce-scatter.4.cloned.1.call-start = ((), (), s32[]{:S(2)}) async-start(), calls=%async_computation.2 | async-start | bytes 2396160
  156.5 2.2 copy-start.5
  156.6 721.3 %copy-start.3 = (f32[256]{0:T(256)S(1)}, f32[256]{0:T(256)}, u32[]{:S(2)}) copy-start(f32[256]{0:T(256)} %param.12) | copy-start | bytes 3076
  600.5 277.9 %copy-start.4 = (f32[65]{0:T(128)}, f32[65]{0:T(128)S(1)}, u32[]{:S(2)}) copy-start(f32[65]{0:T(128)S(1)} %fusion.2) | copy-start | bytes 784
Sparse Core Ops, SparseCore 0:
  150.7 165.8 all-reduce.5
  320.7 245.3 reduce-scatter.3
where the time goes:
time: 886 us; the launch traced here: 885 us
  waiting for transfers between devices  390 us (44%)
  blocking collectives  309 us (35%)
  local copies, waits for them, and re-layouts  141 us (16%)
  other arithmetic  22.2 us (3%)
  between operations  15 us (2%)
    unnamed x4, waiting for transfers between devices  390 us
    unnamed x1, blocking collectives  277 us
    gather x2, local copies, waits for them, and re-layouts, body(): chosen = jnp.take_along_axis(bin_ids, picked, axis=0)  131 us
    psum x1, blocking collectives, body(): local_blocks = lax.psum(partial_blocks, 'feat')  21.7 us
  transfers between devices with their start and end apart: 2, of which 2 were waited for; matrix products, arithmetic and copies ran while one was open for 2% of the time, Pallas kernels for 0%

commit v1 on v0

v1 whole, which is shorter than its diff:
```python
import functools

import jax
import jax.numpy as jnp
from jax import lax
from jax.experimental import pallas as pl
from jax.experimental.pallas import tpu as pltpu
from jax.sharding import PartitionSpec as P

BINS = 256
CORES = 2
HALF = 4
PACK = 40
LANES = 128
SPLIT_REG = 1.0
RIDGE_REG = 1.0
SHRINKAGE = 0.3
MESH = pl.DeviceIdType.MESH
NT = (((1,), (1,)), ((), ()))
NN = (((1,), (0,)), ((), ()))
F32 = jnp.float32
BF16 = jnp.bfloat16


def dot(a, b, dims):
    return lax.dot_general(a, b, dims, preferred_element_type=F32)


def iota(shape, axis):
    return lax.broadcasted_iota(jnp.int32, shape, axis)


def split3(v):
    hi = v.astype(BF16)
    rest = v - hi.astype(F32)
    mid = rest.astype(BF16)
    return hi, mid, (rest - mid.astype(F32)).astype(BF16)


def kernel(
    dims, bins_ref, leaf_ref, grad_ref, hess_ref, raw_ref, prior_ref, elect_ref,
    gain_ref, coef_ref, score_ref,
    xt, chosen, wmat, hist, ring, spread, gathered, xb, wb, lhs,
    parts, gram_z, gram_send, gram_y, square, coef_z, coef_f, tops,
    sx, rx, sring, rring, sh, rh, sgz, rgz, sgy, rgy, scz, rcz, scf, rcf, stp, rtp,
):
    nz, ny, nf = dims
    nx = nf // CORES
    leaves = nz * ny
    rows = leaf_ref.shape[1]
    group = rows // nf
    row_pos = lax.axis_index("rows")
    f = lax.axis_index("feat")
    z, y = row_pos // ny, row_pos % ny
    x, core = f // CORES, f % CORES

    def at_z(k):
        return (lax.rem(z + k + nz, nz) * ny + y, f)

    def at_y(k):
        return (z * ny + lax.rem(y + k + ny, ny), f)

    def at_f(k):
        return (row_pos, lax.rem(f + k + nf, nf))

    started = []

    def send(src, dst, ssem, rsem, dev):
        copy = pltpu.make_async_remote_copy(
            src_ref=src, dst_ref=dst, send_sem=ssem, recv_sem=rsem,
            device_id=dev, device_id_type=MESH,
        )
        copy.start()
        started.append(copy)

    def arrive(dst, ssem, rsem):
        pltpu.make_async_remote_copy(
            src_ref=dst, dst_ref=dst, send_sem=ssem, recv_sem=rsem,
            device_id=(row_pos, f), device_id_type=MESH,
        ).wait_recv()

    barrier = pltpu.get_barrier_semaphore()
    for k in range(1, nf):
        pl.semaphore_signal(barrier, inc=1, device_id=at_f(k), device_id_type=MESH)
    for k in range(1, nz):
        pl.semaphore_signal(barrier, inc=1, device_id=at_z(k), device_id_type=MESH)
    for k in range(1, ny):
        pl.semaphore_signal(barrier, inc=1, device_id=at_y(k), device_id_type=MESH)

    feats = raw_ref.shape[1]
    eye = (iota((feats, feats), 0) == iota((feats, feats), 1)).astype(F32).astype(BF16)
    xt[f] = dot(eye, raw_ref[...], NT)

    leaf = leaf_ref[...]
    grad = grad_ref[...].astype(BF16).astype(F32)
    hess = hess_ref[...].astype(BF16).astype(F32)

    slots = elect_ref.shape[1]
    eye = (iota((slots, slots), 0) == iota((slots, slots), 1)).astype(F32).astype(BF16)
    table = dot(eye, elect_ref[...].astype(F32).astype(BF16), NT).astype(BF16)
    member = (iota((leaves, rows), 0) == leaf).astype(F32).astype(BF16)
    picked = dot(table, member, NN).astype(jnp.int32)
    bins = bins_ref[...]
    number = iota(bins.shape, 0)
    for e in range(slots):
        row = jnp.where(number == picked[e : e + 1, :], bins, 0)
        chosen[e : e + 1, :] = jnp.sum(row, axis=0, keepdims=True).astype(F32)

    pl.semaphore_wait(barrier, (nf - 1) + (nz - 1) + (ny - 1))

    mate = (row_pos, x * CORES + (1 - core))
    for d in range(1, nx):
        dev = (row_pos, lax.rem(x + d, nx) * CORES + core)
        send(xt.at[f], xt.at[f], sx.at[d - 1], rx.at[d - 1], dev)
    send(xt.at[f], xt.at[f], sx.at[nx - 1], rx.at[nx - 1], mate)

    def weigh(d, carry):
        first = leaf == d * ny + iota((ny, rows), 0)
        both = [jnp.where(first, grad, 0.0), jnp.where(first, hess, 0.0)]
        at = pl.multiple_of(d * (2 * ny), 2 * ny)
        wmat[0, pl.ds(at, 2 * ny), :] = jnp.concatenate(both, axis=0).astype(BF16)
        return carry

    lax.fori_loop(0, nz, weigh, 0)

    def weigh_y(d, carry):
        first = leaf == iota((nz, rows), 0) * ny + d
        both = [jnp.where(first, grad, 0.0), jnp.where(first, hess, 0.0)]
        at = pl.multiple_of(d * (2 * nz), 2 * nz)
        wmat[1, pl.ds(at, 2 * nz), :] = jnp.concatenate(both, axis=0).astype(BF16)
        return carry

    lax.fori_loop(0, ny, weigh_y, 0)

    def count(e, carry):
        row = chosen[pl.ds(e, 1), :]
        onehot = (iota((BINS, rows), 0).astype(F32) == row).astype(F32).astype(BF16)
        hist[e] = dot(wmat[e // HALF], onehot, NT)
        return carry

    lax.fori_loop(0, slots, count, 0)

    axes = ((nz, z, at_z, 2 * ny), (ny, y, at_y, 2 * nz))

    def piece(h, part, dest, tall):
        at = pl.multiple_of(dest * tall, tall)
        return hist.at[pl.ds(h * HALF + part * 2, 2), pl.ds(at, tall), :]

    def ring_step(s):
        for h, (n, me, peer, tall) in enumerate(axes):
            far = n // 2
            if s > far:
                continue
            dist = far + 1 - s
            for way, sign in enumerate((1, -1)):
                dest = lax.rem(me + sign * dist + n, n)
                for part in range(2):
                    most = far if part == way else far - 1
                    if dist > most:
                        continue
                    src = piece(h, part, dest, tall)
                    if dist < most:
                        held = ring.at[h, way, part, s - 2]
                        arrive(held, sring.at[h, way, part, s - 2], rring.at[h, way, part, s - 2])
                        held[...] += src[...]
                        src = held
                    send(
                        src, ring.at[h, way, part, s - 1], sring.at[h, way, part, s - 1],
                        rring.at[h, way, part, s - 1], peer(sign),
                    )

    ring_step(1)

    for d in range(1, nx):
        at = lax.rem(x - d + nx, nx) * CORES + core
        arrive(xt.at[at], sx.at[d - 1], rx.at[d - 1])
        send(xt.at[at], xt.at[at], sx.at[nx - 1 + d], rx.at[nx - 1 + d], mate)
    arrive(xt.at[f], sx.at[nx - 1], rx.at[nx - 1])
    for d in range(1, nx):
        at = lax.rem(x - d + nx, nx) * CORES + (1 - core)
        arrive(xt.at[at], sx.at[nx - 1 + d], rx.at[nx - 1 + d])
    for b in range(nf):
        block = xt[b]
        cut = pl.ds(b * group, group)
        scaled = hess_ref[:, cut] * block
        xb[:, cut] = block.astype(BF16)
        wb[0:feats, cut] = scaled.astype(BF16)
        for lz in range(nz):
            mine = leaf_ref[:, cut] == lz * ny + f
            lhs[lz * feats : (lz + 1) * feats, cut] = jnp.where(mine, scaled, 0.0).astype(BF16)
    tail = iota((16, rows), 0)
    wb[feats : feats + 16, :] = jnp.where(
        tail == 0, hess, jnp.where(tail == 1, grad, 0.0)
    ).astype(BF16)
    mine = leaf == iota((nz, rows), 0) * ny + f
    sides = [jnp.where(mine, hess, 0.0), jnp.where(mine, grad, 0.0)]
    if 2 * nz < 16:
        sides.append(jnp.zeros((16 - 2 * nz, rows), F32))
    side = dot(jnp.concatenate(sides, axis=0).astype(BF16), xb[...], NT)
    ones = jnp.concatenate([jnp.where(mine, 1.0, 0.0), jnp.zeros((16 - nz, rows), F32)], axis=0)
    last = dot(ones.astype(BF16), wb[...], NT)
    main = dot(lhs[...], xb[...], NT)
    fold = feats // 2
    for lz in range(nz):
        block = main[lz * feats : (lz + 1) * feats, :]
        parts[lz, 0:fold, :] = jnp.concatenate([block[:fold], block[fold:]], axis=1)
        parts[lz, fold : fold + 8, :] = jnp.zeros((8, LANES), F32)
        parts[lz, fold : fold + 1, 0:feats] = side[lz : lz + 1, :]
        parts[lz, fold + 1 : fold + 2, 0:feats] = side[nz + lz : nz + lz + 1, :]
        parts[lz, fold + 2 : fold + 3, 0 : feats + 16] = last[lz : lz + 1, :]
    for k in range(1, nz):
        to = lax.rem(z + k, nz)
        send(parts.at[to], gram_z.at[k - 1], sgz.at[k - 1], rgz.at[k - 1], at_z(k))

    for s in range(2, max(nz, ny) // 2 + 1):
        ring_step(s)

    total = parts[z]
    for k in range(1, nz):
        arrive(gram_z.at[k - 1], sgz.at[k - 1], rgz.at[k - 1])
        total = total + gram_z[k - 1]
    gram_send[...] = total
    for k in range(1, ny):
        send(gram_send, gram_y.at[k - 1], sgy.at[k - 1], rgy.at[k - 1], at_y(k))

    for h, (n, me, peer, tall) in enumerate(axes):
        other, peer2 = (ny, at_y) if h == 0 else (nz, at_z)
        for part in range(2):
            out = piece(h, part, me, tall)[...]
            for way in range(2):
                far = n // 2 if part == way else n // 2 - 1
                if far > 0:
                    at = (h, way, part, n // 2 - 1)
                    arrive(ring.at[at], sring.at[at], rring.at[at])
                    out = out + ring[at]
            for j in range(2):
                for gh in range(2):
                    slot = gh * HALF + part * 2 + j
                    for d in range(other):
                        spread[h, d, slot : slot + 1, :] = out[j, gh * other + d : gh * other + d + 1, :]
        here = y if h == 0 else z
        for k in range(1, other):
            to = lax.rem(here + k, other)
            send(spread.at[h, to], gathered.at[h, k - 1], sh.at[h, k - 1], rh.at[h, k - 1], peer2(k))

    for k in range(1, ny):
        arrive(gram_y.at[k - 1], sgy.at[k - 1], rgy.at[k - 1])
        total = total + gram_y[k - 1]
    left = iota((fold, LANES), 1) < feats
    square[...] = jnp.zeros((LANES, LANES), F32)
    square[0:fold, :] = jnp.where(left, total[0:fold], 0.0)
    square[fold:feats, :] = jnp.where(left, pltpu.roll(total[0:fold], LANES - feats, 1), 0.0)
    lane = iota((1, LANES), 1)
    ends = total[fold + 2 : fold + 3]
    square[feats : feats + 1, :] = jnp.where(lane < feats, total[fold : fold + 1] + ends, 0.0)
    square[feats + 1 : feats + 2, :] = jnp.where(lane < feats, total[fold + 1 : fold + 2], 0.0)
    square_t = square[...] + jnp.transpose(square[...])
    a = square_t[0:feats]
    lanes = iota((feats, LANES), 1)
    subs = iota((feats, LANES), 0)
    a = jnp.where(lanes <= feats, 0.5 * a, a) + jnp.where(lanes == subs, RIDGE_REG, 0.0)
    border = jnp.broadcast_to(a[:, feats : feats + 1], (feats, LANES))
    for k in range(0, feats, 2):
        c0 = jnp.broadcast_to(a[:, k : k + 1], (feats, LANES))
        c1 = jnp.broadcast_to(a[:, k + 1 : k + 2], (feats, LANES))
        r0, r1 = a[k : k + 1], a[k + 1 : k + 2]
        p00, p10 = c0[k : k + 1], c0[k + 1 : k + 2]
        p01, p11 = c1[k : k + 1], c1[k + 1 : k + 2]
        scale = 1.0 / (p00 * p11 - p01 * p10)
        n0 = (p11 * r0 - p01 * r1) * scale
        n1 = (p00 * r1 - p10 * r0) * scale
        a = a - c0 * n0 - c1 * n1
        a = jnp.where(subs == k, n0, jnp.where(subs == k + 1, n1, a))
    yc = jnp.broadcast_to(a[:, feats : feats + 1], (feats, LANES))
    yb = jnp.broadcast_to(a[:, feats + 1 : feats + 2], (feats, LANES))
    low = ends[:, feats : feats + 1] + RIDGE_REG - jnp.sum(border * yc, axis=0, keepdims=True)
    high = ends[:, feats + 1 : feats + 2] - jnp.sum(border * yb, axis=0, keepdims=True)
    const = high / low
    answer = jnp.sum(jnp.where(lanes == subs, yb - const * yc, 0.0), axis=0, keepdims=True)
    coef_z[z] = -jnp.where(lane == feats, const, answer)
    for k in range(1, nz):
        send(coef_z.at[z], coef_z.at[z], scz.at[k - 1], rcz.at[k - 1], at_z(k))

    upper = (iota((BINS, BINS), 0) <= iota((BINS, BINS), 1)).astype(F32).astype(BF16)
    gains = []
    for h in range(2):
        other = ny if h == 0 else nz
        sums = spread[h, y if h == 0 else z]
        for k in range(1, other):
            arrive(gathered.at[h, k - 1], sh.at[h, k - 1], rh.at[h, k - 1])
            sums = sums + gathered[h, k - 1]
        hi, mid, lo = split3(sums)
        run = dot(hi, upper, NN) + dot(mid, upper, NN) + dot(lo, upper, NN)
        lg, lh = run[0:HALF], run[HALF : 2 * HALF]
        tg, th = lg[:, BINS - 1 : BINS], lh[:, BINS - 1 : BINS]
        rg = tg - lg
        gains.append(
            lg * lg / (lh + SPLIT_REG) + rg * rg / (th - lh + SPLIT_REG) - tg * tg / (th + SPLIT_REG)
        )
    top = jnp.maximum(gains[0], gains[1])
    top = jnp.max(jnp.max(top, axis=1, keepdims=True), axis=0, keepdims=True)
    tops[f] = jnp.broadcast_to(top, (8, LANES))
    for k in range(1, nf):
        send(tops.at[f], tops.at[f], stp.at[k - 1], rtp.at[k - 1], at_f(k))

    for k in range(1, nz):
        at = lax.rem(z - k + nz, nz)
        arrive(coef_z.at[at], scz.at[k - 1], rcz.at[k - 1])
    for k in range(nz):
        coef_f[f, k : k + 1, :] = coef_z[k]
    for k in range(1, nf):
        send(coef_f.at[f], coef_f.at[f], scf.at[k - 1], rcf.at[k - 1], at_f(k))

    for k in range(1, nf):
        at = lax.rem(f - k + nf, nf)
        arrive(tops.at[at], stp.at[k - 1], rtp.at[k - 1])
    best = tops[0]
    for k in range(1, nf):
        best = jnp.maximum(best, tops[k])
    best = best[0:1, 0:1]
    for h in range(2):
        gain_ref[0, h * HALF : (h + 1) * HALF, :] = gains[h] - best

    for k in range(1, nf):
        at = lax.rem(f - k + nf, nf)
        arrive(coef_f.at[at], scf.at[k - 1], rcf.at[k - 1])
    coef_ref[...] = coef_f[y, pl.ds(z, 1), 0 : feats + 1]
    own = leaf_ref[:, pl.ds(pl.multiple_of(f * group, group), group)]
    tables = jnp.concatenate([coef_f[k] for k in range(nf)], axis=0)
    if leaves < LANES:
        tables = jnp.concatenate([tables, jnp.zeros((LANES - leaves, LANES), F32)], axis=0)
    column = jnp.transpose(tables)
    key = lax.rem(own, ny) * nz + own // ny
    pick = (iota((LANES, group), 0) == key).astype(F32).astype(BF16)
    hi, mid, lo = split3(column)
    per_row = dot(hi, pick, NN) + dot(mid, pick, NN) + dot(lo, pick, NN)
    value = jnp.sum(xt[f] * per_row[0:feats], axis=0, keepdims=True) + per_row[feats : feats + 1]
    score_ref[...] = prior_ref[...] + SHRINKAGE * value

    for copy in started:
        copy.wait_send()


def body(bin_ids, leaf_ids, gradient, hessian, raw_feats, prior_score, elected):
    rows = bin_ids.shape[1]
    leaves, slots = elected.shape
    nf = lax.axis_size("feat")
    ny = nf
    nz = lax.axis_size("rows") // ny
    group, feats = raw_feats.shape
    nx = nf // CORES
    far = max(nz, ny)
    tall = 2 * ny
    dma = pltpu.SemaphoreType.DMA
    vmem = pltpu.VMEM
    scratch = [
        vmem((nf, feats, group), F32),
        vmem((slots, rows), F32),
        vmem((2, 2 * leaves, rows), BF16),
        vmem((slots, 2 * leaves, BINS), F32),
        vmem((2, 2, 2, far // 2, 2, tall, BINS), F32),
        vmem((2, far, 2 * HALF, BINS), F32),
        vmem((2, far - 1, 2 * HALF, BINS), F32),
        vmem((feats, rows), BF16),
        vmem((feats + 16, rows), BF16),
        vmem((nz * feats, rows), BF16),
        vmem((nz, PACK, LANES), F32),
        vmem((nz - 1, PACK, LANES), F32),
        vmem((PACK, LANES), F32),
        vmem((ny - 1, PACK, LANES), F32),
        vmem((LANES, LANES), F32),
        vmem((nz, 1, LANES), F32),
        vmem((nf, nz, LANES), F32),
        vmem((nf, 8, LANES), F32),
    ]
    counts = [
        (2 * nx - 1,), (2, 2, 2, far // 2), (2, far - 1), (nz - 1,), (ny - 1,), (nz - 1,),
        (nf - 1,), (nf - 1,),
    ]
    for shape in counts:
        scratch += [dma(shape), dma(shape)]
    gain, coef, score = pl.pallas_call(
        functools.partial(kernel, (nz, ny, nf)),
        out_shape=(
            jax.ShapeDtypeStruct((1, slots, BINS), F32),
            jax.ShapeDtypeStruct((1, feats + 1), F32),
            jax.ShapeDtypeStruct((1, group), F32),
        ),
        in_specs=[pl.BlockSpec(memory_space=pltpu.VMEM)] * 7,
        out_specs=(pl.BlockSpec(memory_space=pltpu.VMEM),) * 3,
        scratch_shapes=scratch,
        compiler_params=pltpu.CompilerParams(
            collective_id=0, has_side_effects=True, vmem_limit_bytes=48 * 1024 * 1024
        ),
        name="level",
    )(
        bin_ids, leaf_ids.reshape(1, rows), gradient.reshape(1, rows), hessian.reshape(1, rows),
        raw_feats, prior_score.reshape(1, group), elected,
    )
    return gain, coef, score.reshape(group)


def solution(mesh):
    in_specs = (
        P("feat", "rows"),
        P("rows"),
        P("rows"),
        P("rows"),
        P(("rows", "feat"), None),
        P(("rows", "feat")),
        P(None, "feat"),
    )
    out_specs = (P("rows", "feat", None), P("rows", None), P(("rows", "feat")))
    return jax.shard_map(body, mesh=mesh, in_specs=in_specs, out_specs=out_specs, check_vma=False)
```

time: 886 us -> 60.8 us (0.07)
  the two profiles are of different devices: /device:TPU:6 before, /device:TPU:1 now
where the time goes in v1:
time: 60.8 us; the launch traced here: 60.5 us
  Pallas kernels  55.7 us (92%)
  local copies, waits for them, and re-layouts  4.17 us (7%)
  between operations  0.69 us (1%)
    pallas_call x1, Pallas kernels, body(): pl.pallas_call(functools.partial(kernel, (nz, ny, nf)), out_shape=(jax.Sh...  55.7 us
    unnamed x19, local copies, waits for them, and re-layouts  4.17 us

profile of v1, /device:TPU:1, one launch (start us, length us, event | category | flops | bytes accessed | tf_op | source)
XLA Modules:
  0.0 60.5 jit_solution(14582870515408023131)
XLA Ops:
  0.6 0.0 copy-start.6
  0.6 0.0 copy-start.5
  0.7 0.7 %copy-done.6 = s32[64,8]{0,1:T(8,128)S(1)} copy-done((s32[64,8]{0,1:T(8,128)S(1)}, s32[64,8]{0,1:T(8,128)}, u32[]{:S(2)}) %copy-start.6) | copy-done | bytes 2072
  1.3 0.1 copy.11.elect_ref
  1.4 0.0 copy-done.5
  1.4 0.0 copy-start.1
  1.4 0.0 copy-start.2
  1.4 0.0 copy-start.3
  1.4 0.0 copy-start.4
  1.4 0.1 copy.10.raw_ref
  1.6 0.5 copy-done.1
  2.1 0.0 copy-done.2
  2.1 0.0 copy-done.3
  2.1 0.0 copy-done.4
  2.1 0.0 copy-start
  2.1 1.0 %copy-done = s32[64,2048]{1,0:T(8,128)S(1)} copy-done((s32[64,2048]{1,0:T(8,128)S(1)}, s32[64,2048]{1,0:T(8,128)}, u32[]{:S(2)}) %copy-start) | copy-done | bytes 524312
  3.2 55.7 %level.1 = (f32[1,8,256]{2,1,0:T(8,128)S(1)}, f32[1,65]{1,0:T(1,128)S(1)}, f32[1,256]{1,0:T(1,128)S(1)}) custom-call(s32[64,2048]{1,0:T(8,128)S(1)} %copy-done, s32[1,2048]{1,0:T(1,128)S(1)} %bitcast.5, f32[1,2048]{1,0:T(1,128)S(1)} %bitcast.6, f32[1,2048]{1,0:T(1,128)S(1)} %bitcast.7, bf16[256,64]{1,0:T(8,128)(2,1)S(1)} %copy.10.raw_ref, ...), custom_call_target="tpu_custom_call" | custom-call | tf_op jit(solution)/shard_map/level/pallas_call | solution.py:382
  58.8 0.6 copy.15
  59.4 0.5 copy.16
  60.0 0.6 copy.17
Async XLA Ops:
  0.6 0.7 %copy-start.6 = (s32[64,8]{0,1:T(8,128)S(1)}, s32[64,8]{0,1:T(8,128)}, u32[]{:S(2)}) copy-start(s32[64,8]{0,1:T(8,128)} %param.13) | copy-start | bytes 6148
  0.6 0.8 %copy-start.5 = (bf16[256,64]{0,1:T(8,128)(2,1)S(1)}, bf16[256,64]{0,1:T(8,128)(2,1)}, u32[]{:S(2)}) copy-start(bf16[256,64]{0,1:T(8,128)(2,1)} %param.11) | copy-start | bytes 98308
  1.4 0.7 %copy-start.1 = (s32[2048]{0:T(1024)S(1)}, s32[2048]{0:T(1024)}, u32[]{:S(2)}) copy-start(s32[2048]{0:T(1024)} %param.8) | copy-start | bytes 24580
  1.4 0.7 %copy-start.2 = (f32[2048]{0:T(1024)S(1)}, f32[2048]{0:T(1024)}, u32[]{:S(2)}) copy-start(f32[2048]{0:T(1024)} %param.9) | copy-start | bytes 24580
  1.4 0.7 %copy-start.3 = (f32[2048]{0:T(1024)S(1)}, f32[2048]{0:T(1024)}, u32[]{:S(2)}) copy-start(f32[2048]{0:T(1024)} %param.10) | copy-start | bytes 24580
  1.4 0.7 %copy-start.4 = (f32[256]{0:T(256)S(1)}, f32[256]{0:T(256)}, u32[]{:S(2)}) copy-start(f32[256]{0:T(256)} %param.12) | copy-start | bytes 3076
  2.1 1.0 %copy-start = (s32[64,2048]{1,0:T(8,128)S(1)}, s32[64,2048]{1,0:T(8,128)}, u32[]{:S(2)}) copy-start(s32[64,2048]{1,0:T(8,128)} %bins_ref.1) | copy-start | bytes 1572868

commit v2 on v1

--- a/solution.py
+++ b/solution.py
@@ -10,7 +10,7 @@
 BINS = 256
 CORES = 2
 HALF = 4
-PACK = 40
+PACK = 24
 LANES = 128
 SPLIT_REG = 1.0
 RIDGE_REG = 1.0
@@ -38,9 +38,10 @@
 
 
 def kernel(
-    dims, bins_ref, leaf_ref, grad_ref, hess_ref, raw_ref, prior_ref, elect_ref,
+    dims, bins_hbm, leaf_hbm, grad_hbm, hess_hbm, raw_hbm, prior_hbm, elect_hbm,
     gain_ref, coef_ref, score_ref,
-    xt, chosen, wmat, hist, ring, spread, gathered, xb, wb, lhs,
+    bins_ref, leaf_ref, grad_ref, hess_ref, raw_ref, prior_ref, elect_ref, load_sem,
+    xt, chosen, wmat, hist, ring, spread, gathered, xb, lhs,
     parts, gram_z, gram_send, gram_y, square, coef_z, coef_f, tops,
     sx, rx, sring, rring, sh, rh, sgz, rgz, sgy, rgy, scz, rcz, scf, rcf, stp, rtp,
 ):
@@ -48,6 +49,8 @@
     nx = nf // CORES
     leaves = nz * ny
     rows = leaf_ref.shape[1]
+    feats = raw_ref.shape[0]
+    slots = elect_ref.shape[0]
     group = rows // nf
     row_pos = lax.axis_index("rows")
     f = lax.axis_index("feat")
@@ -65,19 +68,27 @@
 
     started = []
 
-    def send(src, dst, ssem, rsem, dev):
+    def send(src, dst, sems, dev):
         copy = pltpu.make_async_remote_copy(
-            src_ref=src, dst_ref=dst, send_sem=ssem, recv_sem=rsem,
+            src_ref=src, dst_ref=dst, send_sem=sems[0].at[sems[2]], recv_sem=sems[1].at[sems[2]],
             device_id=dev, device_id_type=MESH,
         )
         copy.start()
         started.append(copy)
 
-    def arrive(dst, ssem, rsem):
+    def arrive(dst, sems):
         pltpu.make_async_remote_copy(
-            src_ref=dst, dst_ref=dst, send_sem=ssem, recv_sem=rsem,
+            src_ref=dst, dst_ref=dst, send_sem=sems[0].at[sems[2]], recv_sem=sems[1].at[sems[2]],
             device_id=(row_pos, f), device_id_type=MESH,
         ).wait_recv()
+
+    pairs = (
+        (raw_hbm, raw_ref), (leaf_hbm, leaf_ref), (elect_hbm, elect_ref), (bins_hbm, bins_ref),
+        (grad_hbm, grad_ref), (hess_hbm, hess_ref), (prior_hbm, prior_ref),
+    )
+    loads = [pltpu.make_async_copy(a, b, load_sem.at[i]) for i, (a, b) in enumerate(pairs)]
+    for load in loads:
+        load.start()
 
     barrier = pltpu.get_barrier_semaphore()
     for k in range(1, nf):
@@ -87,17 +98,21 @@
     for k in range(1, ny):
         pl.semaphore_signal(barrier, inc=1, device_id=at_y(k), device_id_type=MESH)
 
-    feats = raw_ref.shape[1]
-    eye = (iota((feats, feats), 0) == iota((feats, feats), 1)).astype(F32).astype(BF16)
-    xt[f] = dot(eye, raw_ref[...], NT)
-
+    loads[0].wait()
+    xt[f] = raw_ref[...].astype(F32)
+    pl.semaphore_wait(barrier, (nf - 1) + (nz - 1) + (ny - 1))
+    mate = (row_pos, x * CORES + (1 - core))
+    for d in range(1, nx):
+        dev = (row_pos, lax.rem(x + d, nx) * CORES + core)
+        send(xt.at[f], xt.at[f], (sx, rx, (d - 1,)), dev)
+    send(xt.at[f], xt.at[f], (sx, rx, (nx - 1,)), mate)
+
+    for load in loads[1:]:
+        load.wait()
     leaf = leaf_ref[...]
     grad = grad_ref[...].astype(BF16).astype(F32)
     hess = hess_ref[...].astype(BF16).astype(F32)
-
-    slots = elect_ref.shape[1]
-    eye = (iota((slots, slots), 0) == iota((slots, slots), 1)).astype(F32).astype(BF16)
-    table = dot(eye, elect_ref[...].astype(F32).astype(BF16), NT).astype(BF16)
+    table = elect_ref[...].astype(F32).astype(BF16)
     member = (iota((leaves, rows), 0) == leaf).astype(F32).astype(BF16)
     picked = dot(table, member, NN).astype(jnp.int32)
     bins = bins_ref[...]
@@ -106,14 +121,6 @@
         row = jnp.where(number == picked[e : e + 1, :], bins, 0)
         chosen[e : e + 1, :] = jnp.sum(row, axis=0, keepdims=True).astype(F32)
 
-    pl.semaphore_wait(barrier, (nf - 1) + (nz - 1) + (ny - 1))
-
-    mate = (row_pos, x * CORES + (1 - core))
-    for d in range(1, nx):
-        dev = (row_pos, lax.rem(x + d, nx) * CORES + core)
-        send(xt.at[f], xt.at[f], sx.at[d - 1], rx.at[d - 1], dev)
-    send(xt.at[f], xt.at[f], sx.at[nx - 1], rx.at[nx - 1], mate)
-
     def weigh(d, carry):
         first = leaf == d * ny + iota((ny, rows), 0)
         both = [jnp.where(first, grad, 0.0), jnp.where(first, hess, 0.0)]
@@ -130,15 +137,14 @@
         wmat[1, pl.ds(at, 2 * nz), :] = jnp.concatenate(both, axis=0).astype(BF16)
         return carry
 
-    lax.fori_loop(0, ny, weigh_y, 0)
+    one, zero = jnp.ones((), BF16), jnp.zeros((), BF16)
 
     def count(e, carry):
         row = chosen[pl.ds(e, 1), :]
-        onehot = (iota((BINS, rows), 0).astype(F32) == row).astype(F32).astype(BF16)
+        number = iota((BINS, rows), 0).astype(F32).astype(BF16)
+        onehot = jnp.where(number == row.astype(BF16), one, zero)
         hist[e] = dot(wmat[e // HALF], onehot, NT)
         return carry
-
-    lax.fori_loop(0, slots, count, 0)
 
     axes = ((nz, z, at_z, 2 * ny), (ny, y, at_y, 2 * nz))
 
@@ -146,8 +152,9 @@
         at = pl.multiple_of(dest * tall, tall)
         return hist.at[pl.ds(h * HALF + part * 2, 2), pl.ds(at, tall), :]
 
-    def ring_step(s):
-        for h, (n, me, peer, tall) in enumerate(axes):
+    def ring_step(s, halves=(0, 1)):
+        for h in halves:
+            n, me, peer, tall = axes[h]
             far = n // 2
             if s > far:
                 continue
@@ -161,67 +168,85 @@
                     src = piece(h, part, dest, tall)
                     if dist < most:
                         held = ring.at[h, way, part, s - 2]
-                        arrive(held, sring.at[h, way, part, s - 2], rring.at[h, way, part, s - 2])
+                        arrive(held, (sring, rring, (h, way, part, s - 2)))
                         held[...] += src[...]
                         src = held
-                    send(
-                        src, ring.at[h, way, part, s - 1], sring.at[h, way, part, s - 1],
-                        rring.at[h, way, part, s - 1], peer(sign),
-                    )
-
-    ring_step(1)
+                    at = (h, way, part, s - 1)
+                    send(src, ring.at[at], (sring, rring, at), peer(sign))
+
+    lax.fori_loop(0, HALF, count, 0)
+    ring_step(1, (0,))
+    lax.fori_loop(0, ny, weigh_y, 0)
+    lax.fori_loop(HALF, slots, count, 0)
+    ring_step(1, (1,))
 
     for d in range(1, nx):
         at = lax.rem(x - d + nx, nx) * CORES + core
-        arrive(xt.at[at], sx.at[d - 1], rx.at[d - 1])
-        send(xt.at[at], xt.at[at], sx.at[nx - 1 + d], rx.at[nx - 1 + d], mate)
-    arrive(xt.at[f], sx.at[nx - 1], rx.at[nx - 1])
+        arrive(xt.at[at], (sx, rx, (d - 1,)))
+        send(xt.at[at], xt.at[at], (sx, rx, (nx - 1 + d,)), mate)
+    steps = max(nz, ny) // 2
+    ring_step(2, (0,))
+    arrive(xt.at[f], (sx, rx, (nx - 1,)))
     for d in range(1, nx):
         at = lax.rem(x - d + nx, nx) * CORES + (1 - core)
-        arrive(xt.at[at], sx.at[nx - 1 + d], rx.at[nx - 1 + d])
+        arrive(xt.at[at], (sx, rx, (nx - 1 + d,)))
     for b in range(nf):
         block = xt[b]
         cut = pl.ds(b * group, group)
+        cut2 = pl.ds(rows + b * group, group)
         scaled = hess_ref[:, cut] * block
         xb[:, cut] = block.astype(BF16)
-        wb[0:feats, cut] = scaled.astype(BF16)
+        xb[:, cut2] = scaled.astype(BF16)
         for lz in range(nz):
             mine = leaf_ref[:, cut] == lz * ny + f
             lhs[lz * feats : (lz + 1) * feats, cut] = jnp.where(mine, scaled, 0.0).astype(BF16)
-    tail = iota((16, rows), 0)
-    wb[feats : feats + 16, :] = jnp.where(
-        tail == 0, hess, jnp.where(tail == 1, grad, 0.0)
-    ).astype(BF16)
+            lhs[lz * feats : (lz + 1) * feats, cut2] = jnp.where(mine, block, 0.0).astype(BF16)
     mine = leaf == iota((nz, rows), 0) * ny + f
-    sides = [jnp.where(mine, hess, 0.0), jnp.where(mine, grad, 0.0)]
-    if 2 * nz < 16:
-        sides.append(jnp.zeros((16 - 2 * nz, rows), F32))
-    side = dot(jnp.concatenate(sides, axis=0).astype(BF16), xb[...], NT)
-    ones = jnp.concatenate([jnp.where(mine, 1.0, 0.0), jnp.zeros((16 - nz, rows), F32)], axis=0)
-    last = dot(ones.astype(BF16), wb[...], NT)
+    side_h = jnp.where(mine, hess, 0.0)
+    side_g = jnp.where(mine, grad, 0.0)
+    sides = jnp.concatenate([side_h, side_g], axis=0).astype(BF16)
+    ones = jnp.concatenate([jnp.where(mine, 1.0, 0.0), jnp.zeros((nz, rows), F32)], axis=0)
+    side = dot(sides, xb[:, 0:rows], NT) + dot(ones.astype(BF16), xb[:, rows : 2 * rows], NT)
+    sum_h = jnp.sum(side_h, axis=1, keepdims=True)
+    sum_g = jnp.sum(side_g, axis=1, keepdims=True)
     main = dot(lhs[...], xb[...], NT)
     fold = feats // 2
+    quarter = fold // 2
+    low_half = iota((fold, feats), 0) >= iota((fold, feats), 1) + 1
+    on_diag = iota((fold, feats), 0) == iota((fold, feats), 1)
+    lane = iota((1, LANES), 1)
     for lz in range(nz):
         block = main[lz * feats : (lz + 1) * feats, :]
-        parts[lz, 0:fold, :] = jnp.concatenate([block[:fold], block[fold:]], axis=1)
-        parts[lz, fold : fold + 8, :] = jnp.zeros((8, LANES), F32)
-        parts[lz, fold : fold + 1, 0:feats] = side[lz : lz + 1, :]
-        parts[lz, fold + 1 : fold + 2, 0:feats] = side[nz + lz : nz + lz + 1, :]
-        parts[lz, fold + 2 : fold + 3, 0 : feats + 16] = last[lz : lz + 1, :]
+        corner = jnp.concatenate([block[fold:, fold:], block[fold:, :fold]], axis=1)
+        tri = jnp.where(low_half, corner, block[:fold])
+        diag = jnp.sum(jnp.where(on_diag, corner, 0.0), axis=0, keepdims=True)
+        parts[lz, 0:quarter, :] = jnp.concatenate([tri[:quarter], tri[quarter:]], axis=1)
+        parts[lz, quarter : quarter + 1, :] = jnp.concatenate(
+            [side[lz : lz + 1, :], side[nz + lz : nz + lz + 1, :]], axis=1
+        )
+        ends = jnp.where(lane == feats, sum_h[lz : lz + 1], 0.0)
+        ends = jnp.where(lane == feats + 1, sum_g[lz : lz + 1], ends)
+        parts[lz, quarter + 1 : quarter + 2, :] = ends
+        parts[lz, quarter + 1 : quarter + 2, 0:feats] = diag
+        parts[lz, quarter + 2 : quarter + 8, :] = jnp.zeros((6, LANES), F32)
     for k in range(1, nz):
         to = lax.rem(z + k, nz)
-        send(parts.at[to], gram_z.at[k - 1], sgz.at[k - 1], rgz.at[k - 1], at_z(k))
-
-    for s in range(2, max(nz, ny) // 2 + 1):
+        send(parts.at[to], gram_z.at[k - 1], (sgz, rgz, (k - 1,)), at_z(k))
+
+    ring_step(2, (1,))
+    for s in range(3, steps):
         ring_step(s)
 
     total = parts[z]
     for k in range(1, nz):
-        arrive(gram_z.at[k - 1], sgz.at[k - 1], rgz.at[k - 1])
+        arrive(gram_z.at[k - 1], (sgz, rgz, (k - 1,)))
         total = total + gram_z[k - 1]
     gram_send[...] = total
     for k in range(1, ny):
-        send(gram_send, gram_y.at[k - 1], sgy.at[k - 1], rgy.at[k - 1], at_y(k))
+        send(gram_send, gram_y.at[k - 1], (sgy, rgy, (k - 1,)), at_y(k))
+
+    if steps > 2:
+        ring_step(steps)
 
     for h, (n, me, peer, tall) in enumerate(axes):
         other, peer2 = (ny, at_y) if h == 0 else (nz, at_z)
@@ -231,7 +256,7 @@
                 far = n // 2 if part == way else n // 2 - 1
                 if far > 0:
                     at = (h, way, part, n // 2 - 1)
-                    arrive(ring.at[at], sring.at[at], rring.at[at])
+                    arrive(ring.at[at], (sring, rring, at))
                     out = out + ring[at]
             for j in range(2):
                 for gh in range(2):
@@ -241,19 +266,31 @@
         here = y if h == 0 else z
         for k in range(1, other):
             to = lax.rem(here + k, other)
-            send(spread.at[h, to], gathered.at[h, k - 1], sh.at[h, k - 1], rh.at[h, k - 1], peer2(k))
+            send(spread.at[h, to], gathered.at[h, k - 1], (sh, rh, (h, k - 1)), peer2(k))
 
     for k in range(1, ny):
-        arrive(gram_y.at[k - 1], sgy.at[k - 1], rgy.at[k - 1])
+        arrive(gram_y.at[k - 1], (sgy, rgy, (k - 1,)))
         total = total + gram_y[k - 1]
-    left = iota((fold, LANES), 1) < feats
+    subs = iota((fold, LANES), 0)
+    lanes = iota((fold, LANES), 1)
+    turned = pltpu.roll(total[0:quarter], LANES - feats, 1)
+    tri = jnp.concatenate([total[0:quarter], turned], axis=0)
+    ends = total[quarter + 1 : quarter + 2]
     square[...] = jnp.zeros((LANES, LANES), F32)
-    square[0:fold, :] = jnp.where(left, total[0:fold], 0.0)
-    square[fold:feats, :] = jnp.where(left, pltpu.roll(total[0:fold], LANES - feats, 1), 0.0)
-    lane = iota((1, LANES), 1)
-    ends = total[fold + 2 : fold + 3]
-    square[feats : feats + 1, :] = jnp.where(lane < feats, total[fold : fold + 1] + ends, 0.0)
-    square[feats + 1 : feats + 2, :] = jnp.where(lane < feats, total[fold + 1 : fold + 2], 0.0)
+    square[0:fold, :] = jnp.where(
+        (lanes > subs) & (lanes < feats), tri, jnp.where(lanes == subs, 0.5 * tri, 0.0)
+    )
+    shifted = pltpu.roll(tri, fold, 1)
+    far_diag = jnp.broadcast_to(pltpu.roll(ends, fold, 1), (fold, LANES))
+    square[fold:feats, :] = jnp.where(
+        (lanes >= fold) & (lanes < subs + fold), shifted,
+        jnp.where(lanes == subs + fold, 0.5 * far_diag, 0.0),
+    )
+    edge = total[quarter : quarter + 1]
+    square[feats : feats + 1, :] = jnp.where(lane < feats, edge, 0.0)
+    square[feats + 1 : feats + 2, :] = jnp.where(
+        lane < feats, pltpu.roll(edge, LANES - feats, 1), 0.0
+    )
     square_t = square[...] + jnp.transpose(square[...])
     a = square_t[0:feats]
     lanes = iota((feats, LANES), 1)
@@ -279,7 +316,7 @@
     answer = jnp.sum(jnp.where(lanes == subs, yb - const * yc, 0.0), axis=0, keepdims=True)
     coef_z[z] = -jnp.where(lane == feats, const, answer)
     for k in range(1, nz):
-        send(coef_z.at[z], coef_z.at[z], scz.at[k - 1], rcz.at[k - 1], at_z(k))
+        send(coef_z.at[z], coef_z.at[z], (scz, rcz, (k - 1,)), at_z(k))
 
     upper = (iota((BINS, BINS), 0) <= iota((BINS, BINS), 1)).astype(F32).astype(BF16)
     gains = []
@@ -287,7 +324,7 @@
         other = ny if h == 0 else nz
         sums = spread[h, y if h == 0 else z]
         for k in range(1, other):
-            arrive(gathered.at[h, k - 1], sh.at[h, k - 1], rh.at[h, k - 1])
+            arrive(gathered.at[h, k - 1], (sh, rh, (h, k - 1)))
             sums = sums + gathered[h, k - 1]
         hi, mid, lo = split3(sums)
         run = dot(hi, upper, NN) + dot(mid, upper, NN) + dot(lo, upper, NN)
@@ -301,19 +338,19 @@
     top = jnp.max(jnp.max(top, axis=1, keepdims=True), axis=0, keepdims=True)
     tops[f] = jnp.broadcast_to(top, (8, LANES))
     for k in range(1, nf):
-        send(tops.at[f], tops.at[f], stp.at[k - 1], rtp.at[k - 1], at_f(k))
+        send(tops.at[f], tops.at[f], (stp, rtp, (k - 1,)), at_f(k))
 
     for k in range(1, nz):
         at = lax.rem(z - k + nz, nz)
-        arrive(coef_z.at[at], scz.at[k - 1], rcz.at[k - 1])
+        arrive(coef_z.at[at], (scz, rcz, (k - 1,)))
     for k in range(nz):
         coef_f[f, k : k + 1, :] = coef_z[k]
     for k in range(1, nf):
-        send(coef_f.at[f], coef_f.at[f], scf.at[k - 1], rcf.at[k - 1], at_f(k))
+        send(coef_f.at[f], coef_f.at[f], (scf, rcf, (k - 1,)), at_f(k))
 
     for k in range(1, nf):
         at = lax.rem(f - k + nf, nf)
-        arrive(tops.at[at], stp.at[k - 1], rtp.at[k - 1])
+        arrive(tops.at[at], (stp, rtp, (k - 1,)))
     best = tops[0]
     for k in range(1, nf):
         best = jnp.maximum(best, tops[k])
@@ -323,7 +360,7 @@
 
     for k in range(1, nf):
         at = lax.rem(f - k + nf, nf)
-        arrive(coef_f.at[at], scf.at[k - 1], rcf.at[k - 1])
+        arrive(coef_f.at[at], (scf, rcf, (k - 1,)))
     coef_ref[...] = coef_f[y, pl.ds(z, 1), 0 : feats + 1]
     own = leaf_ref[:, pl.ds(pl.multiple_of(f * group, group), group)]
     tables = jnp.concatenate([coef_f[k] for k in range(nf)], axis=0)
@@ -348,12 +385,16 @@
     ny = nf
     nz = lax.axis_size("rows") // ny
     group, feats = raw_feats.shape
+    small = lambda width, kind: pltpu.VMEM((1, width), kind)
     nx = nf // CORES
     far = max(nz, ny)
     tall = 2 * ny
     dma = pltpu.SemaphoreType.DMA
     vmem = pltpu.VMEM
     scratch = [
+        vmem((bin_ids.shape[0], rows), jnp.int32),
+        small(rows, jnp.int32), small(rows, F32), small(rows, F32),
+        vmem((feats, group), BF16), small(group, F32), vmem((slots, leaves), jnp.int32), dma((7,)),
         vmem((nf, feats, group), F32),
         vmem((slots, rows), F32),
         vmem((2, 2 * leaves, rows), BF16),
@@ -361,9 +402,8 @@
         vmem((2, 2, 2, far // 2, 2, tall, BINS), F32),
         vmem((2, far, 2 * HALF, BINS), F32),
         vmem((2, far - 1, 2 * HALF, BINS), F32),
-        vmem((feats, rows), BF16),
-        vmem((feats + 16, rows), BF16),
-        vmem((nz * feats, rows), BF16),
+        vmem((feats, 2 * rows), BF16),
+        vmem((nz * feats, 2 * rows), BF16),
         vmem((nz, PACK, LANES), F32),
         vmem((nz - 1, PACK, LANES), F32),
         vmem((PACK, LANES), F32),
@@ -386,16 +426,16 @@
             jax.ShapeDtypeStruct((1, feats + 1), F32),
             jax.ShapeDtypeStruct((1, group), F32),
         ),
-        in_specs=[pl.BlockSpec(memory_space=pltpu.VMEM)] * 7,
+        in_specs=[pl.BlockSpec(memory_space=pltpu.HBM)] * 7,
         out_specs=(pl.BlockSpec(memory_space=pltpu.VMEM),) * 3,
         scratch_shapes=scratch,
         compiler_params=pltpu.CompilerParams(
-            collective_id=0, has_side_effects=True, vmem_limit_bytes=48 * 1024 * 1024
+            collective_id=0, has_side_effects=True, vmem_limit_bytes=66_000_000
         ),
         name="level",
     )(
         bin_ids, leaf_ids.reshape(1, rows), gradient.reshape(1, rows), hessian.reshape(1, rows),
-        raw_feats, prior_score.reshape(1, group), elected,
+        raw_feats.T, prior_score.reshape(1, group), elected.T,
     )
     return gain, coef, score.reshape(group)
 

time: 60.8 us -> 52.8 us (0.87)
  Pallas kernels: 55.7 us -> 49.5 us
  local copies, waits for them, and re-layouts: 4.17 us -> 2.5 us
    pallas_call x1, Pallas kernels: 55.7 us -> 49.5 us  [body(): pl.pallas_call(functools.partial(kernel, (nz, ny, nf)), out_shape=(jax.Sh...]
    unnamed x19 -> x7, local copies, waits for them, and re-layouts: 4.17 us -> 2.5 us
where the time goes in v2:
time: 52.8 us; the launch traced here: 52.7 us
  Pallas kernels  49.5 us (94%)
  local copies, waits for them, and re-layouts  2.5 us (5%)
  between operations  0.65 us (1%)
    pallas_call x1, Pallas kernels, body(): pl.pallas_call(functools.partial(kernel, (nz, ny, nf)), out_shape=(jax.Sh...  49.5 us
    unnamed x7, local copies, waits for them, and re-layouts  2.5 us

profile of v2, /device:TPU:1, one launch (start us, length us, event | category | flops | bytes accessed | tf_op | source)
XLA Modules:
  0.0 52.7 jit_solution(10565377488890880418)
XLA Ops:
  0.6 49.5 %level.1 = (f32[1,8,256]{2,1,0:T(8,128)}, f32[1,65]{1,0:T(1,128)}, f32[1,256]{1,0:T(1,128)}) custom-call(s32[64,2048]{1,0:T(8,128)} %bins_hbm.1, s32[1,2048]{1,0:T(1,128)} %bitcast.8, f32[1,2048]{1,0:T(1,128)} %bitcast.9, f32[1,2048]{1,0:T(1,128)} %bitcast.10, bf16[64,256]{1,0:T(8,128)(2,1)} %bitcast.7, f32[1,256]{1,0:T(1,128)} %bitcast.12, s32[8,64]{1,0:T(8,128)} %bitcast.11), custom_call_target="tpu_custom_call" | custom-call | tf_op jit(solution)/shard_map/level/pallas_call | solution.py:422
  50.1 0.0 copy-start.1
  50.2 1.3 %copy.13 = f32[1,8,256]{2,1,0:T(8,128)} copy(f32[1,8,256]{2,1,0:T(8,128)} %get-tuple-element.12) | data formatting | bytes 16384
  51.5 0.0 copy-done.1
  51.5 0.0 copy-start
  51.5 0.5 copy.14
  52.0 0.1 copy-done
  52.1 0.6 %copy.15 = f32[256]{0:T(256)} copy(f32[256]{0:T(256)S(1)} %bitcast.13) | data formatting | bytes 2048
Async XLA Ops:
  50.1 1.3 %copy-start.1 = (f32[1,65]{1,0:T(1,128)S(1)}, f32[1,65]{1,0:T(1,128)}, u32[]{:S(2)}) copy-start(f32[1,65]{1,0:T(1,128)} %get-tuple-element.13) | copy-start | bytes 784
  51.5 0.6 %copy-start = (f32[1,256]{1,0:T(1,128)S(1)}, f32[1,256]{1,0:T(1,128)}, u32[]{:S(2)}) copy-start(f32[1,256]{1,0:T(1,128)} %get-tuple-element.8) | copy-start | bytes 3076

commit v3 on v2

--- a/solution.py
+++ b/solution.py
@@ -11,6 +11,7 @@
 CORES = 2
 HALF = 4
 PACK = 24
+SUB = 16
 LANES = 128
 SPLIT_REG = 1.0
 RIDGE_REG = 1.0
@@ -40,10 +41,10 @@
 def kernel(
     dims, bins_hbm, leaf_hbm, grad_hbm, hess_hbm, raw_hbm, prior_hbm, elect_hbm,
     gain_ref, coef_ref, score_ref,
-    bins_ref, leaf_ref, grad_ref, hess_ref, raw_ref, prior_ref, elect_ref, load_sem,
-    xt, chosen, wmat, hist, ring, spread, gathered, xb, lhs,
-    parts, gram_z, gram_send, gram_y, square, coef_z, coef_f, tops,
-    sx, rx, sring, rring, sh, rh, sgz, rgz, sgy, rgy, scz, rcz, scf, rcf, stp, rtp,
+    bins_ref, leaf_ref, grad_ref, hess_ref, raw_ref, prior_ref, elect_ref, load_sem, entered,
+    xt, sifted, chosen, wmat, hist, ring, spread, gathered, xb,
+    parts, gram_z, gram_send, gram_y, square, coef_z, tops,
+    sx, rx, sring, rring, sh, rh, sgz, rgz, sgy, rgy, scz, rcz, stp, rtp,
 ):
     nz, ny, nf = dims
     nx = nf // CORES
@@ -91,21 +92,35 @@
         load.start()
 
     barrier = pltpu.get_barrier_semaphore()
+    beside = (at_z(1), at_z(-1), at_y(1), at_y(-1))
+    for dev in beside:
+        pl.semaphore_signal(barrier, inc=1, device_id=dev, device_id_type=MESH)
     for k in range(1, nf):
         pl.semaphore_signal(barrier, inc=1, device_id=at_f(k), device_id_type=MESH)
-    for k in range(1, nz):
-        pl.semaphore_signal(barrier, inc=1, device_id=at_z(k), device_id_type=MESH)
-    for k in range(1, ny):
-        pl.semaphore_signal(barrier, inc=1, device_id=at_y(k), device_id_type=MESH)
+
+    rounds = max(nz, ny) // 2 - 1
+
+    def heard(r):
+        if 0 <= r < rounds:
+            for i in range(2):
+                pl.semaphore_wait(entered.at[r, i], 2)
+
+    def pass_on(r):
+        heard(r - 1)
+        if r < rounds:
+            for i, dev in enumerate(beside):
+                pl.semaphore_signal(entered.at[r, i // 2], inc=1, device_id=dev, device_id_type=MESH)
 
     loads[0].wait()
     xt[f] = raw_ref[...].astype(F32)
-    pl.semaphore_wait(barrier, (nf - 1) + (nz - 1) + (ny - 1))
+    pl.semaphore_wait(barrier, (nf - 1) + len(beside))
     mate = (row_pos, x * CORES + (1 - core))
     for d in range(1, nx):
         dev = (row_pos, lax.rem(x + d, nx) * CORES + core)
         send(xt.at[f], xt.at[f], (sx, rx, (d - 1,)), dev)
     send(xt.at[f], xt.at[f], (sx, rx, (nx - 1,)), mate)
+
+    pass_on(0)
 
     for load in loads[1:]:
         load.wait()
@@ -114,12 +129,19 @@
     hess = hess_ref[...].astype(BF16).astype(F32)
     table = elect_ref[...].astype(F32).astype(BF16)
     member = (iota((leaves, rows), 0) == leaf).astype(F32).astype(BF16)
-    picked = dot(table, member, NN).astype(jnp.int32)
-    bins = bins_ref[...]
-    number = iota(bins.shape, 0)
+    picked = dot(table, member, NN)
+    one, zero = jnp.ones((), BF16), jnp.zeros((), BF16)
+    bins = bins_ref[...].astype(F32).astype(BF16)
+    ahead = iota((SUB, rows), 0)
     for e in range(slots):
-        row = jnp.where(number == picked[e : e + 1, :], bins, 0)
-        chosen[e : e + 1, :] = jnp.sum(row, axis=0, keepdims=True).astype(F32)
+        row = picked[e : e + 1, :].astype(BF16)
+        held = zero
+        for g in range(bins.shape[0] // SUB):
+            number = (ahead + g * SUB).astype(F32).astype(BF16)
+            held = jnp.where(number == row, bins[g * SUB : (g + 1) * SUB], held)
+        sifted[e * SUB : (e + 1) * SUB, :] = held
+    gather_rows = iota((slots, slots * SUB), 1) // SUB == iota((slots, slots * SUB), 0)
+    chosen[...] = dot(gather_rows.astype(F32).astype(BF16), sifted[...], NN)
 
     def weigh(d, carry):
         first = leaf == d * ny + iota((ny, rows), 0)
@@ -136,8 +158,6 @@
         at = pl.multiple_of(d * (2 * nz), 2 * nz)
         wmat[1, pl.ds(at, 2 * nz), :] = jnp.concatenate(both, axis=0).astype(BF16)
         return carry
-
-    one, zero = jnp.ones((), BF16), jnp.zeros((), BF16)
 
     def count(e, carry):
         row = chosen[pl.ds(e, 1), :]
@@ -176,9 +196,24 @@
 
     lax.fori_loop(0, HALF, count, 0)
     ring_step(1, (0,))
+    pass_on(1)
     lax.fori_loop(0, ny, weigh_y, 0)
     lax.fori_loop(HALF, slots, count, 0)
     ring_step(1, (1,))
+    pass_on(2)
+
+    parts[...] = jnp.zeros_like(parts)
+    edge = iota((SUB, rows), 0)
+    xb[feats : feats + SUB, 0:rows] = jnp.where(edge == 0, 1.0, 0.0).astype(BF16)
+    xb[feats : feats + SUB, rows : 2 * rows] = jnp.where(
+        edge == 0, hess, jnp.where(edge == 1, grad, 0.0)
+    ).astype(BF16)
+    in_leaf = [jnp.where(leaf == lz * ny + f, 1.0, 0.0).astype(BF16) for lz in range(nz)]
+    mine = leaf == iota((nz, rows), 0) * ny + f
+    sum_h = jnp.sum(jnp.where(mine, hess, 0.0), axis=1, keepdims=True)
+    sum_g = jnp.sum(jnp.where(mine, grad, 0.0), axis=1, keepdims=True)
+    at_lane = iota((nz, LANES), 1)
+    ends = jnp.where(at_lane == feats, sum_h, jnp.where(at_lane == feats + 1, sum_g, 0.0))
 
     for d in range(1, nx):
         at = lax.rem(x - d + nx, nx) * CORES + core
@@ -195,40 +230,33 @@
         cut = pl.ds(b * group, group)
         cut2 = pl.ds(rows + b * group, group)
         scaled = hess_ref[:, cut] * block
-        xb[:, cut] = block.astype(BF16)
-        xb[:, cut2] = scaled.astype(BF16)
-        for lz in range(nz):
-            mine = leaf_ref[:, cut] == lz * ny + f
-            lhs[lz * feats : (lz + 1) * feats, cut] = jnp.where(mine, scaled, 0.0).astype(BF16)
-            lhs[lz * feats : (lz + 1) * feats, cut2] = jnp.where(mine, block, 0.0).astype(BF16)
-    mine = leaf == iota((nz, rows), 0) * ny + f
-    side_h = jnp.where(mine, hess, 0.0)
-    side_g = jnp.where(mine, grad, 0.0)
-    sides = jnp.concatenate([side_h, side_g], axis=0).astype(BF16)
-    ones = jnp.concatenate([jnp.where(mine, 1.0, 0.0), jnp.zeros((nz, rows), F32)], axis=0)
-    side = dot(sides, xb[:, 0:rows], NT) + dot(ones.astype(BF16), xb[:, rows : 2 * rows], NT)
-    sum_h = jnp.sum(side_h, axis=1, keepdims=True)
-    sum_g = jnp.sum(side_g, axis=1, keepdims=True)
-    main = dot(lhs[...], xb[...], NT)
+        xb[0:feats, cut] = block.astype(BF16)
+        xb[0:feats, cut2] = scaled.astype(BF16)
+    right = [jnp.concatenate([xb[0:feats, rows:] * m, xb[0:feats, :rows] * m], axis=1) for m in in_leaf]
+    wide = dot(xb[...], jnp.concatenate(right, axis=0), NT)
     fold = feats // 2
     quarter = fold // 2
-    low_half = iota((fold, feats), 0) >= iota((fold, feats), 1) + 1
-    on_diag = iota((fold, feats), 0) == iota((fold, feats), 1)
+    span = (fold, nz * feats)
+    behind = lax.rem(iota(span, 1), feats) - iota(span, 0)
+    corner = pltpu.roll(wide[fold:feats], nz * feats - fold, 1)
+    tri = jnp.where(behind < 0, corner, wide[0:fold])
+    diag = jnp.sum(jnp.where(behind == 0, corner, 0.0), axis=0, keepdims=True)
+    first = iota((1, LANES), 1) < feats
     lane = iota((1, LANES), 1)
-    for lz in range(nz):
-        block = main[lz * feats : (lz + 1) * feats, :]
-        corner = jnp.concatenate([block[fold:, fold:], block[fold:, :fold]], axis=1)
-        tri = jnp.where(low_half, corner, block[:fold])
-        diag = jnp.sum(jnp.where(on_diag, corner, 0.0), axis=0, keepdims=True)
-        parts[lz, 0:quarter, :] = jnp.concatenate([tri[:quarter], tri[quarter:]], axis=1)
-        parts[lz, quarter : quarter + 1, :] = jnp.concatenate(
-            [side[lz : lz + 1, :], side[nz + lz : nz + lz + 1, :]], axis=1
-        )
-        ends = jnp.where(lane == feats, sum_h[lz : lz + 1], 0.0)
-        ends = jnp.where(lane == feats + 1, sum_g[lz : lz + 1], ends)
-        parts[lz, quarter + 1 : quarter + 2, :] = ends
-        parts[lz, quarter + 1 : quarter + 2, 0:feats] = diag
-        parts[lz, quarter + 2 : quarter + 8, :] = jnp.zeros((6, LANES), F32)
+    for t in range(nz // 2):
+        cut = slice(t * LANES, (t + 1) * LANES)
+        upper, lower = tri[0:quarter, cut], tri[quarter:fold, cut]
+        edge = wide[feats : feats + 8, cut]
+        turned = pltpu.roll(edge, feats, 1)
+        even, odd = 2 * t, 2 * t + 1
+        parts[even, 0:quarter, :] = jnp.where(first, upper, pltpu.roll(lower, feats, 1))
+        parts[odd, 0:quarter, :] = jnp.where(first, pltpu.roll(upper, feats, 1), lower)
+        parts[even, quarter : quarter + 1, :] = jnp.where(first, edge[0:1], turned[1:2])
+        parts[odd, quarter : quarter + 1, :] = jnp.where(first, turned[0:1], edge[1:2])
+        here = diag[:, cut]
+        for lz, row in ((even, here), (odd, pltpu.roll(here, feats, 1))):
+            parts[lz, quarter + 1 : quarter + 2, :] = jnp.where(first, row, ends[lz : lz + 1])
+    heard(2)
     for k in range(1, nz):
         to = lax.rem(z + k, nz)
         send(parts.at[to], gram_z.at[k - 1], (sgz, rgz, (k - 1,)), at_z(k))
@@ -314,9 +342,30 @@
     high = ends[:, feats + 1 : feats + 2] - jnp.sum(border * yb, axis=0, keepdims=True)
     const = high / low
     answer = jnp.sum(jnp.where(lanes == subs, yb - const * yc, 0.0), axis=0, keepdims=True)
-    coef_z[z] = -jnp.where(lane == feats, const, answer)
-    for k in range(1, nz):
-        send(coef_z.at[z], coef_z.at[z], (scz, rcz, (k - 1,)), at_z(k))
+    early = list(started)
+    started.clear()
+    own = f * nz + z
+    coef_z[own] = -jnp.where(lane == feats, const, answer)
+
+    def give(k, carry):
+        dz = lax.rem(lax.div(k, nf) + nz // 2, nz)
+        df = lax.rem(lax.rem(k, nf) + nf // 2, nf)
+
+        @pl.when(dz + df > 0)
+        def _():
+            dev = (lax.rem(z + dz, nz) * ny + y, lax.rem(f + df, nf))
+            pltpu.make_async_remote_copy(
+                src_ref=coef_z.at[own], dst_ref=coef_z.at[own], send_sem=scz.at[0], recv_sem=rcz.at[0],
+                device_id=dev, device_id_type=MESH,
+            ).start()
+
+        return carry
+
+    lax.fori_loop(0, nz * nf, give, 0)
+    shared = pltpu.make_async_remote_copy(
+        src_ref=coef_z.at[pl.ds(0, nz * nf - 1)], dst_ref=coef_z.at[pl.ds(0, nz * nf - 1)],
+        send_sem=scz.at[0], recv_sem=rcz.at[0], device_id=(row_pos, f), device_id_type=MESH,
+    )
 
     upper = (iota((BINS, BINS), 0) <= iota((BINS, BINS), 1)).astype(F32).astype(BF16)
     gains = []
@@ -340,13 +389,8 @@
     for k in range(1, nf):
         send(tops.at[f], tops.at[f], (stp, rtp, (k - 1,)), at_f(k))
 
-    for k in range(1, nz):
-        at = lax.rem(z - k + nz, nz)
-        arrive(coef_z.at[at], (scz, rcz, (k - 1,)))
-    for k in range(nz):
-        coef_f[f, k : k + 1, :] = coef_z[k]
-    for k in range(1, nf):
-        send(coef_f.at[f], coef_f.at[f], (scf, rcf, (k - 1,)), at_f(k))
+    for copy in early:
+        copy.wait_send()
 
     for k in range(1, nf):
         at = lax.rem(f - k + nf, nf)
@@ -358,16 +402,14 @@
     for h in range(2):
         gain_ref[0, h * HALF : (h + 1) * HALF, :] = gains[h] - best
 
-    for k in range(1, nf):
-        at = lax.rem(f - k + nf, nf)
-        arrive(coef_f.at[at], (scf, rcf, (k - 1,)))
-    coef_ref[...] = coef_f[y, pl.ds(z, 1), 0 : feats + 1]
-    own = leaf_ref[:, pl.ds(pl.multiple_of(f * group, group), group)]
-    tables = jnp.concatenate([coef_f[k] for k in range(nf)], axis=0)
+    shared.wait_recv()
+    coef_ref[...] = coef_z[y * nz + z][:, 0 : feats + 1]
+    own_rows = leaf_ref[:, pl.ds(pl.multiple_of(f * group, group), group)]
+    tables = jnp.concatenate([coef_z[k] for k in range(nz * nf)], axis=0)
     if leaves < LANES:
         tables = jnp.concatenate([tables, jnp.zeros((LANES - leaves, LANES), F32)], axis=0)
     column = jnp.transpose(tables)
-    key = lax.rem(own, ny) * nz + own // ny
+    key = lax.rem(own_rows, ny) * nz + own_rows // ny
     pick = (iota((LANES, group), 0) == key).astype(F32).astype(BF16)
     hi, mid, lo = split3(column)
     per_row = dot(hi, pick, NN) + dot(mid, pick, NN) + dot(lo, pick, NN)
@@ -376,6 +418,7 @@
 
     for copy in started:
         copy.wait_send()
+    shared.wait_send()
 
 
 def body(bin_ids, leaf_ids, gradient, hessian, raw_feats, prior_score, elected):
@@ -395,27 +438,27 @@
         vmem((bin_ids.shape[0], rows), jnp.int32),
         small(rows, jnp.int32), small(rows, F32), small(rows, F32),
         vmem((feats, group), BF16), small(group, F32), vmem((slots, leaves), jnp.int32), dma((7,)),
+        pltpu.SemaphoreType.REGULAR((max(nz, ny) // 2 - 1, 2)),
         vmem((nf, feats, group), F32),
+        vmem((slots * SUB, rows), BF16),
         vmem((slots, rows), F32),
         vmem((2, 2 * leaves, rows), BF16),
         vmem((slots, 2 * leaves, BINS), F32),
         vmem((2, 2, 2, far // 2, 2, tall, BINS), F32),
         vmem((2, far, 2 * HALF, BINS), F32),
         vmem((2, far - 1, 2 * HALF, BINS), F32),
-        vmem((feats, 2 * rows), BF16),
-        vmem((nz * feats, 2 * rows), BF16),
+        vmem((feats + SUB, 2 * rows), BF16),
         vmem((nz, PACK, LANES), F32),
         vmem((nz - 1, PACK, LANES), F32),
         vmem((PACK, LANES), F32),
         vmem((ny - 1, PACK, LANES), F32),
         vmem((LANES, LANES), F32),
-        vmem((nz, 1, LANES), F32),
-        vmem((nf, nz, LANES), F32),
+        vmem((nz * nf, 1, LANES), F32),
         vmem((nf, 8, LANES), F32),
     ]
     counts = [
-        (2 * nx - 1,), (2, 2, 2, far // 2), (2, far - 1), (nz - 1,), (ny - 1,), (nz - 1,),
-        (nf - 1,), (nf - 1,),
+        (2 * nx - 1,), (2, 2, 2, far // 2), (2, far - 1), (nz - 1,), (ny - 1,), (1,),
+        (nf - 1,),
     ]
     for shape in counts:
         scratch += [dma(shape), dma(shape)]

time: 52.8 us -> 49.1 us (0.930)
  Pallas kernels: 49.5 us -> 45.8 us
    pallas_call x1, Pallas kernels: 49.5 us -> 45.8 us  [body(): pl.pallas_call(functools.partial(kernel, (nz, ny, nf)), out_shape=(jax.Sh...]
where the time goes in v3:
time: 49.1 us; the launch traced here: 48.9 us
  Pallas kernels  45.8 us (93%)
  local copies, waits for them, and re-layouts  2.5 us (5%)
  between operations  0.65 us (1%)
    pallas_call x1, Pallas kernels, body(): pl.pallas_call(functools.partial(kernel, (nz, ny, nf)), out_shape=(jax.Sh...  45.8 us
    unnamed x7, local copies, waits for them, and re-layouts  2.5 us

profile of v3, /device:TPU:1, one launch (start us, length us, event | category | flops | bytes accessed | tf_op | source)
XLA Modules:
  0.0 48.9 jit_solution(17280023011515981407)
XLA Ops:
  0.6 45.8 %level.1 = (f32[1,8,256]{2,1,0:T(8,128)}, f32[1,65]{1,0:T(1,128)}, f32[1,256]{1,0:T(1,128)}) custom-call(s32[64,2048]{1,0:T(8,128)} %bins_hbm.1, s32[1,2048]{1,0:T(1,128)} %bitcast.8, f32[1,2048]{1,0:T(1,128)} %bitcast.9, f32[1,2048]{1,0:T(1,128)} %bitcast.10, bf16[64,256]{1,0:T(8,128)(2,1)} %bitcast.7, f32[1,256]{1,0:T(1,128)} %bitcast.12, s32[8,64]{1,0:T(8,128)} %bitcast.11), custom_call_target="tpu_custom_call" | custom-call | tf_op jit(solution)/shard_map/level/pallas_call | solution.py:465
  46.4 0.0 copy-start.1
  46.4 1.3 %copy.13 = f32[1,8,256]{2,1,0:T(8,128)} copy(f32[1,8,256]{2,1,0:T(8,128)} %get-tuple-element.12) | data formatting | bytes 16384
  47.7 0.0 copy-done.1
  47.7 0.0 copy-start
  47.7 0.5 %copy.14 = f32[1,65]{1,0:T(1,128)} copy(f32[1,65]{1,0:T(1,128)S(1)} %copy-done.1) | data formatting | bytes 520
  48.2 0.1 copy-done
  48.4 0.6 %copy.15 = f32[256]{0:T(256)} copy(f32[256]{0:T(256)S(1)} %bitcast.13) | data formatting | bytes 2048
Async XLA Ops:
  46.4 1.3 %copy-start.1 = (f32[1,65]{1,0:T(1,128)S(1)}, f32[1,65]{1,0:T(1,128)}, u32[]{:S(2)}) copy-start(f32[1,65]{1,0:T(1,128)} %get-tuple-element.13) | copy-start | bytes 784
  47.7 0.6 %copy-start = (f32[1,256]{1,0:T(1,128)S(1)}, f32[1,256]{1,0:T(1,128)}, u32[]{:S(2)}) copy-start(f32[1,256]{1,0:T(1,128)} %get-tuple-element.8) | copy-start | bytes 3076

commit v4 on v3

--- a/solution.py
+++ b/solution.py
@@ -421,6 +421,14 @@
     shared.wait_send()
 
 
+def place(*refs):
+    copies = [pltpu.make_async_copy(refs[i], refs[3 + i], refs[6].at[i]) for i in range(3)]
+    for copy in copies:
+        copy.start()
+    for copy in copies:
+        copy.wait()
+
+
 def body(bin_ids, leaf_ids, gradient, hessian, raw_feats, prior_score, elected):
     rows = bin_ids.shape[1]
     leaves, slots = elected.shape
@@ -462,6 +470,11 @@
     ]
     for shape in counts:
         scratch += [dma(shape), dma(shape)]
+    operands = (
+        bin_ids, leaf_ids.reshape(1, rows), gradient.reshape(1, rows), hessian.reshape(1, rows),
+        raw_feats.T, prior_score.reshape(1, group), elected.T,
+    )
+    operands = [pltpu.with_memory_space_constraint(v, pltpu.HBM) for v in operands]
     gain, coef, score = pl.pallas_call(
         functools.partial(kernel, (nz, ny, nf)),
         out_shape=(
@@ -473,13 +486,21 @@
         out_specs=(pl.BlockSpec(memory_space=pltpu.VMEM),) * 3,
         scratch_shapes=scratch,
         compiler_params=pltpu.CompilerParams(
-            collective_id=0, has_side_effects=True, vmem_limit_bytes=66_000_000
+            collective_id=0, has_side_effects=True, vmem_limit_bytes=50331648
         ),
         name="level",
     )(
-        bin_ids, leaf_ids.reshape(1, rows), gradient.reshape(1, rows), hessian.reshape(1, rows),
-        raw_feats.T, prior_score.reshape(1, group), elected.T,
-    )
+        *operands
+    )
+    results = [pltpu.with_memory_space_constraint(v, pltpu.VMEM) for v in (gain, coef, score)]
+    gain, coef, score = pl.pallas_call(
+        place,
+        out_shape=tuple(jax.ShapeDtypeStruct(r.shape, r.dtype) for r in results),
+        in_specs=[pl.BlockSpec(memory_space=pltpu.VMEM)] * 3,
+        out_specs=(pl.BlockSpec(memory_space=pltpu.HBM),) * 3,
+        scratch_shapes=[dma((3,))],
+        name="place",
+    )(*results)
     return gain, coef, score.reshape(group)
 
 

time: 49.1 us -> 46.6 us (0.949)
  local copies, waits for them, and re-layouts: 2.5 us -> 0 us
    unnamed x7 -> x0, local copies, waits for them, and re-layouts: 2.5 us -> none
    pallas_call x0 -> x1, Pallas kernels: none -> 0.63 us  [body(): pl.pallas_call(place, out_shape=tuple((jax.ShapeDtypeStruct(r.shape, r.dt...]
    pallas_call x1, Pallas kernels: 45.8 us -> 45.2 us  [body(): pl.pallas_call(functools.partial(kernel, (nz, ny, nf)), out_shape=(jax.Sh...]
where the time goes in v4:
time: 46.6 us; the launch traced here: 46.5 us
  Pallas kernels  45.8 us (98%)
  between operations  0.64 us (1%)
    pallas_call x1, Pallas kernels, body(): pl.pallas_call(functools.partial(kernel, (nz, ny, nf)), out_shape=(jax.Sh...  45.2 us

profile of v4, /device:TPU:1, one launch (start us, length us, event | category | flops | bytes accessed | tf_op | source)
XLA Modules:
  0.0 46.5 jit_solution(3160179706482894239)
XLA Ops:
  0.6 45.2 %level.1 = (f32[1,8,256]{2,1,0:T(8,128)S(1)}, f32[1,65]{1,0:T(1,128)S(1)}, f32[1,256]{1,0:T(1,128)S(1)}) custom-call(s32[64,2048]{1,0:T(8,128)} %bins_hbm.1, s32[1,2048]{1,0:T(1,128)} %bitcast.8, f32[1,2048]{1,0:T(1,128)} %bitcast.9, f32[1,2048]{1,0:T(1,128)} %bitcast.10, bf16[64,256]{1,0:T(8,128)(2,1)} %bitcast.7, f32[1,256]{1,0:T(1,128)} %bitcast.12, ...), custom_call_target="tpu_custom_call" | custom-call | tf_op jit(solution)/shard_map/level/pallas_call | solution.py:478
  45.8 0.6 %place.1 = (f32[1,8,256]{2,1,0:T(8,128)}, f32[1,65]{1,0:T(1,128)}, f32[1,256]{1,0:T(1,128)}) custom-call(f32[1,8,256]{2,1,0:T(8,128)S(1)} %get-tuple-element.9.refs_0_, f32[1,65]{1,0:T(1,128)S(1)} %get-tuple-element.10.refs_1_, f32[1,256]{1,0:T(1,128)S(1)} %get-tuple-element.11.refs_2_), custom_call_target="tpu_custom_call" | custom-call | tf_op jit(solution)/shard_map/place/pallas_call | solution.py:496
